TPU v7x, 128 devices: a whole 4x4x4 slice. The times are simulated.
128 devices in a mesh: chan: 16 (over z, y), grp: 8 (over x, core).
Axes of the slice: x: 4, y: 4, z: 4, core: 2. Of those that a mesh axis runs over, the one named last changes fastest.
Arguments:
- voltages: bfloat16 [512, 2, 139, 1024], P(('chan', 'grp')), may hold values from -6 to 6
- filter_taps: float32 [12, 512], replicated, may hold values from -1.75 to 1.75
- chan_index: int32 [192], replicated, may hold values from 0 to 511
- beam_weights: bfloat16 [192, 4096, 2, 512], P('chan', 'grp'), may hold values from -0.1875 to 0.1875
Outputs:
- beams: bfloat16 [192, 4096, 2, 2, 128], P('chan', 'grp')
Inputs may be any that keep to these rules, and one draw needn't show every extreme that they name: `chan_index`: filterbank channel numbers; a channel may be selected more than once.
All inputs are finite; a program needn't handle non-finite values.
Results may differ from a plain program's by a relative error of at most 0.0065.
Values may be sent and summed in bfloat16 or wider, within the bound.
A program may use at most 192 MiB of HBM per device.

v0:
```python
import math

import jax
import jax.numpy as jnp
from jax import lax
from jax.sharding import PartitionSpec as P


def build_table(chan_index, fft_size):
    position = jnp.arange(fft_size, dtype=jnp.int32)
    phase = position[:, None] * chan_index[None, :] % fft_size
    angle = 2.0 * math.pi / fft_size * phase.astype(jnp.float32)
    factor = 1.0 / math.sqrt(fft_size)
    cosine = jnp.cos(angle) * factor
    sine = jnp.sin(angle) * factor
    upper = jnp.concatenate([cosine, -sine], axis=1)
    lower = jnp.concatenate([sine, cosine], axis=1)
    return jnp.concatenate([upper, lower], axis=0).astype(jnp.bfloat16)


def channelize(voltages, filter_taps, phase_table):
    tap_count = filter_taps.shape[0]
    spectra_count = voltages.shape[2] - tap_count + 1
    doubled = jnp.concatenate([filter_taps, filter_taps], axis=1)
    filtered = jnp.zeros(voltages.shape[:2] + (spectra_count, voltages.shape[3]), jnp.float32)
    for tap_delay in range(tap_count):
        window = voltages[:, :, tap_delay : tap_delay + spectra_count, :].astype(jnp.float32)
        filtered = filtered + window * doubled[tap_delay]
    filtered = filtered.astype(jnp.bfloat16)
    flat = filtered.reshape(-1, filtered.shape[3])
    result = jnp.dot(flat, phase_table, preferred_element_type=jnp.float32).astype(jnp.bfloat16)
    return result.reshape(voltages.shape[:2] + (spectra_count, 2, phase_table.shape[1] // 2))


def shards(voltages, filter_taps, chan_index, beam_weights):
    fft_size = filter_taps.shape[1]
    phase_table = build_table(chan_index, fft_size)
    spectra = channelize(voltages, filter_taps, phase_table)
    gathered = lax.all_gather(spectra, "grp", axis=0, tiled=True)
    turned = lax.all_to_all(gathered, "chan", split_axis=4, concat_axis=0, tiled=True)
    partial_value = jnp.einsum(
        "cbws,spmrc->cbwprm", beam_weights, turned, preferred_element_type=jnp.float32
    )
    real_part = partial_value[:, :, 0, :, 0] - partial_value[:, :, 1, :, 1]
    imag_part = partial_value[:, :, 0, :, 1] + partial_value[:, :, 1, :, 0]
    return jnp.stack([real_part, imag_part], axis=3).astype(jnp.bfloat16)


def solution(mesh):
    placed = (P(("chan", "grp"), None, None, None), P(), P(), P("chan", "grp", None, None))
    return jax.shard_map(
        shards,
        mesh=mesh,
        in_specs=placed,
        out_specs=P("chan", "grp", None, None, None),
        check_vma=False,
    )
```

profile of v0, /device:TPU:1, one launch (start us, length us, event | category | flops | bytes accessed | tf_op | source)
XLA Modules:
  0.0 247.0 jit_solution(4974403950366790959)
XLA Ops:
  6.5 0.0 all-gather.2.cloned.1.call-start
  6.5 0.8 constant_dynamic-update-slice_fusion.1
  7.3 0.8 constant_dynamic-update-slice_fusion
  8.1 3.8 %negate_convert_fusion = (bf16[512,192]{1,0:T(8,128)(2,1)}, bf16[512,192]{1,0:T(8,128)(2,1)}, bf16[512,192]{1,0:T(8,128)(2,1)}) fusion(s32[192]{0:T(256)} %param.6), kind=kLoop, calls=%fused_computation.28 | loop fusion | flops 1966080 | bytes 590592 | tf_op jit(solution)/shard_map/convert.9
  11.9 26.8 %fusion.26 = (bf16[4,2,128,1024]{3,1,2,0:T(2,128)(2,1)S(1)}, bf16[4,2,128,1024]{3,1,2,0:T(2,128)(2,1)S(1)}, bf16[4,2,128,1024]{3,1,2,0:T(2,128)(2,1)S(1)}, bf16[...) fusion(bf16[4,2,139,1024]{3,1,2,0:T(2,128)(2,1)} %param.4), kind=kLoop, calls=%fused_computation.38 | loop fusion | bytes 50331648 | tf_op jit(solution)/shard_map/slice | solution.py:27
  38.7 8.3 %add_convert_fusion = bf16[4,2,128,1024]{3,2,1,0:T(8,128)(2,1)S(1)} fusion(bf16[4,2,128,1024]{3,1,2,0:T(2,128)(2,1)S(1)} %get-tuple-element.16, bf16[4,2,128,1024]{3,1,2,0:T(2,128)(2,1)S(1)} %get-tuple-element.6, bf16[4,2,128,1024]{3,1,2,0:T(2,128)(2,1)S(1)} %get-tuple-element.7, bf16[4,2,128,1024]{3,1,2,0:T(2,128)(2,1)S(1)} %get-tuple-element.8, ...), kind=kLoop, calls=%fused_computation.11 | loop fusion | flops 37748736 | bytes 27312128 | tf_op jit(solution)/shard_map/convert_element_type | solution.py:29
  47.0 3.4 %convolution_convert_fusion = bf16[1024,384]{1,0:T(8,128)(2,1)} fusion(bf16[1024,1024]{1,0:T(8,128)(2,1)S(1)} %bitcast.46, bf16[512,192]{1,0:T(8,128)(2,1)} %get-tuple-element.31, bf16[512,192]{1,0:T(8,128)(2,1)} %get-tuple-element.30, bf16[512,192]{1,0:T(8,128)(2,1)} %get-tuple-element.29), kind=kOutput, calls=%fused_computation.14 | convolution fusion | flops 808845312 | bytes 3473408 | tf_op jit(solution)/shard_map/dot_general | solution.py:31
  50.4 1.4 copy.42
  51.8 1.4 reshape.58
  53.2 0.0 all-gather.2.cloned.1.call-update
  53.3 48.1 %all-gather.2.cloned.1.call-done = bf16[32,2,128,2,192]{2,1,0,4,3:T(2,128)(2,1)} async-done(((bf16[4,2,128,2,192]{2,1,0,4,3:T(2,128)(2,1)}), bf16[32,2,128,2,192]{2,1,0,4,3:T(2,128)(2,1)}) %all-gather.2.cloned.1.call-update) | async-done | bytes 6291472 | tf_op jit(solution)/shard_map/all_gather | solution.py:39
  101.4 7.1 %copy.43 = bf16[32,2,128,2,192]{2,1,0,3,4:T(2,128)(2,1)S(1)} copy(bf16[32,2,128,2,192]{2,1,0,4,3:T(2,128)(2,1)} %all-gather.2.cloned.1.call-done) | data formatting | bytes 12582912 | tf_op jit(solution)/shard_map/all_gather | solution.py:39
  108.5 79.1 %all_to_all.18 = bf16[32,2,128,2,192]{2,1,0,3,4:T(2,128)(2,1)S(1)} all-to-all(bf16[32,2,128,2,192]{2,1,0,3,4:T(2,128)(2,1)S(1)} %copy.43), channel_id=1, replica_groups=mesh['chan'=16,'grp'=8] {'chan'}, dimensions={4} | all-to-all | bytes 12582912 | tf_op jit(solution)/shard_map/all_to_all | solution.py:40
  187.6 1.0 copy.44
  188.6 4.6 %copy.45 = bf16[16,32,2,128,2,12]{3,1,0,5,4,2:T(8,128)(2,1)} copy(bf16[16,32,2,128,2,12]{3,1,5,0,4,2:T(8,128)(2,1)S(1)} %bitcast.43) | data formatting | bytes 12582912 | tf_op jit(solution)/shard_map/all_to_all | solution.py:40
  193.1 16.0 %fusion.2 = f32[12,512,2,2,2,128]{1,5,2,4,3,0:T(8,128)} fusion(bf16[12,512,2,512,1,1]{3,2,1,0,5,4:T(2,128)(2,1)} %bitcast.45, bf16[512,2,128,2,12,1]{2,0,4,3,1,5:T(8,128)(2,1)} %bitcast.44), kind=kOutput, calls=%fused_computation.2 | convolution fusion | flops 6442450944 | bytes 44040192 | tf_op jit(solution)/shard_map/cbws,spmrc->cbwprm/dot_general | solution.py:41
  209.1 5.8 %fusion.10 = bf16[12,512,2,1,128]{1,4,2,0,3:T(8,128)(2,1)S(1)} fusion(f32[12,512,2,2,2,128]{1,5,2,4,3,0:T(8,128)} %fusion.2), kind=kLoop, calls=%fused_computation.13 | loop fusion | flops 3145728 | bytes 15728640 | tf_op jit(solution)/shard_map/add | solution.py:45
  214.9 5.9 %fusion.9 = bf16[12,512,2,1,128]{1,4,2,0,3:T(8,128)(2,1)S(1)} fusion(f32[12,512,2,2,2,128]{1,5,2,4,3,0:T(8,128)} %fusion.2), kind=kLoop, calls=%fused_computation.12 | loop fusion | flops 3145728 | bytes 15728640 | tf_op jit(solution)/shard_map/sub | solution.py:44
  220.8 3.2 %pad_maximum_fusion = bf16[12,512,2,2,128]{1,4,2,0,3:T(8,128)(2,1)} fusion(bf16[12,512,2,1,128]{1,4,2,0,3:T(8,128)(2,1)S(1)} %fusion.10, bf16[12,512,2,1,128]{1,4,2,0,3:T(8,128)(2,1)S(1)} %fusion.9), kind=kLoop, calls=%fused_computation.9 | loop fusion | flops 3145728 | bytes 12582912 | tf_op jit(solution)/shard_map/stack | solution.py:46
  224.0 16.2 %copy.50 = bf16[12,512,2,2,128]{4,3,2,1,0:T(2,128)(2,1)} copy(bf16[12,512,2,2,128]{1,4,2,0,3:T(8,128)(2,1)} %pad_maximum_fusion) | data formatting | bytes 12582912 | tf_op jit(solution)/shard_map/stack | solution.py:46
  (1 shorter events, 0.0 us)
Async XLA Ops:
  6.5 94.9 %all-gather.2.cloned.1.call-start = ((), (), s32[]{:S(2)}) async-start(), calls=%async_computation.1 | async-start | bytes 7077888 | tf_op jit(solution)/shard_map/all_gather | solution.py:39
Sparse Core Ops, SparseCore 0:
  53.4 47.9 all-gather.1
where the time goes:
time: 248 us; the launch traced here: 247 us
  blocking collectives  79.1 us (32%)
  local copies, waits for them, and re-layouts  60 us (24%)
  waiting for transfers between devices  48.2 us (19%)
  other arithmetic  26.9 us (11%)
  matrix products  19.4 us (8%)
  between operations  13.4 us (5%)
    all_to_all x1, blocking collectives, shards(): lax.all_to_all(gathered, 'chan', split_axis=4, concat_axis=0, tiled=True)  79.1 us
    all_gather x1, waiting for transfers between devices, shards(): gathered = lax.all_gather(spectra, 'grp', axis=0, tiled=True)  48.1 us
    slice x1, local copies, waits for them, and re-layouts, channelize(): voltages[:, :, tap_delay:tap_delay + spectra_count, :].astype(jnp.float32)  26.8 us
    another operation x1, local copies, waits for them, and re-layouts, shards(): return jnp.stack([real_part, imag_part], axis=3).astype(jnp.bfloat16)  16.2 us
    dot_general x1, matrix products, shards(): jnp.einsum('cbws,spmrc->cbwprm', beam_weights, turned, preferred_element_...  16 us
    convert_element_type x1, other arithmetic, channelize(): filtered = filtered.astype(jnp.bfloat16)  8.28 us
    all_gather x1, local copies, waits for them, and re-layouts, shards(): gathered = lax.all_gather(spectra, 'grp', axis=0, tiled=True)  7.05 us
    sub x1, other arithmetic, shards(): real_part = partial_value[:, :, 0, :, 0] - partial_value[:, :, 1, :, 1]  5.9 us
  transfers between devices with their start and end apart: 1, of which 1 were waited for; matrix products, arithmetic and copies ran while one was open for 0% of the time, Pallas kernels for 0%

commit v1 on v0

v1 whole, which is shorter than its diff:
```python
import functools
import math

import jax
import jax.numpy as jnp
import numpy as np
from jax import lax
from jax.experimental import pallas as pl
from jax.experimental.pallas import tpu as pltpu
from jax.sharding import PartitionSpec as P

MESH = pl.DeviceIdType.MESH
LANES = 128
CHUNKS = 4


def fourier_rows(size):
    steps = np.arange(size, dtype=np.int64)
    phase = (steps[:, None] * steps[None, :]) % size
    angle = np.float32(2.0 * math.pi / size) * phase.astype(np.float32)
    factor = np.float32(1.0 / math.sqrt(size))
    rows = np.concatenate([np.cos(angle) * factor, np.sin(angle) * factor], axis=1)
    return rows.astype(jnp.bfloat16)


def spectra_kernel(
    dims, volts_hbm, taps_ref, index_ref, rows_ref, out_ref,
    volts, tapb, table, sums, flat, spread, ready,
    load_sem, own_sem, one_send, one_recv, side_send, side_recv, far_send, far_recv, mate_send, mate_recv,
):
    n_chan, n_x, stations, pols, blocks, taps, size, channels = dims
    n_grp = 2 * n_x
    spectra = blocks - taps + 1
    tiles = size // LANES
    per = channels // n_chan
    step = per // CHUNKS
    quads = 2 * pols
    rows_m = 2 * tiles * pols

    chan = lax.axis_index("chan")
    grp = lax.axis_index("grp")
    place = grp // 2
    core = grp % 2
    right = lax.rem(place + 1, n_x) * 2 + core
    left = lax.rem(place + n_x - 1, n_x) * 2 + core
    across = lax.rem(place + 2, n_x) * 2 + core
    mate = place * 2 + 1 - core

    def load(s):
        span = pl.ds(s * blocks * rows_m, blocks * rows_m)
        return pltpu.make_async_copy(volts_hbm.at[span], volts.at[span], load_sem.at[s])

    for s in range(stations):
        load(s).start()

    barrier = pltpu.get_barrier_semaphore()

    def greet(j, carry):
        other = lax.rem(chan + j, n_chan)
        pl.semaphore_signal(barrier, inc=1, device_id={"chan": other, "grp": grp}, device_id_type=MESH)
        return carry

    lax.fori_loop(1, n_chan, greet, 0)
    for other in (right, left, mate):
        pl.semaphore_signal(barrier, inc=1, device_id={"chan": chan, "grp": other}, device_id_type=MESH)

    for t in range(taps):
        for tile in range(tiles):
            line = taps_ref[pl.ds(t, 1), pl.ds(tile * LANES, LANES)]
            tapb[pl.ds((t * tiles + tile) * pols, pols), :] = jnp.broadcast_to(line, (pols, LANES))

    place_of = lax.broadcasted_iota(jnp.int32, (channels, size), 1)
    chosen = (place_of == index_ref[...]).astype(jnp.float32).astype(jnp.bfloat16)
    picked = jnp.dot(chosen, rows_ref[...], preferred_element_type=jnp.float32)
    table[pl.ds(0, channels), :] = picked.astype(jnp.bfloat16)
    table[pl.ds(channels, channels), pl.ds(0, size)] = (-picked[:, size:]).astype(jnp.bfloat16)
    table[pl.ds(channels, channels), pl.ds(size, size)] = picked[:, :size].astype(jnp.bfloat16)

    group = 8
    half = tiles * pols
    for s in range(stations):
        load(s).wait()

        def filter_group(i, carry):
            first = i * group
            coefs = [tapb[pl.ds(t * half, half), :] for t in range(taps)]
            views = []
            for m in range(group + taps - 1):
                start = pl.multiple_of((s * blocks + first + m) * rows_m, rows_m)
                views.append(volts[pl.ds(start, rows_m), :].astype(jnp.float32))
            for m in range(group):
                for part in range(2):
                    total = None
                    for t in range(taps):
                        term = views[m + t][part * half : (part + 1) * half] * coefs[t]
                        total = term if total is None else total + term
                    at = pl.multiple_of((first + m) * rows_m, rows_m) + part * half
                    sums[pl.ds(at, half), :] = total
            return carry

        lax.fori_loop(0, spectra // group, filter_group, 0)
        for p in range(pols):
            for part in range(2):
                for tile in range(tiles):
                    line = part * half + tile * pols + p
                    flat[pl.ds(p * spectra, spectra), pl.ds((part * tiles + tile) * LANES, LANES)] = sums[
                        pl.ds(line, spectra, stride=rows_m), :
                    ].astype(jnp.bfloat16)
        product = lax.dot_general(
            table[...], flat[...], (((1,), (1,)), ((), ())), preferred_element_type=jnp.float32
        )
        for p in range(pols):
            for part in range(2):
                spread[pl.ds((p * 2 + part) * stations + s, channels, stride=quads * stations), :] = product[
                    part * channels : (part + 1) * channels, p * spectra : (p + 1) * spectra
                ]

    packed = ready.reshape(channels * quads * stations, LANES)

    def pack(k, carry):
        wide = spread[pl.ds(pl.multiple_of(k * 64, 64), 64), :].astype(jnp.bfloat16)
        packed[pl.ds(pl.multiple_of(k * 64, 64), 64), :] = wide
        return carry

    lax.fori_loop(0, channels * quads * stations // 64, pack, 0)

    outgoing = ready.reshape(n_chan, per, quads, stations, LANES)
    pl.semaphore_wait(barrier, n_chan + 2)

    def span(i):
        return pl.ds(i * step, step)

    def first_copy(i, other):
        return pltpu.make_async_remote_copy(
            src_ref=outgoing.at[other, span(i)],
            dst_ref=out_ref.at[span(i), :, chan, grp],
            send_sem=one_send.at[i],
            recv_sem=one_recv.at[i],
            device_id={"chan": other, "grp": grp},
            device_id_type=MESH,
        )

    def own_copy(i):
        return pltpu.make_async_copy(outgoing.at[chan, span(i)], out_ref.at[span(i), :, chan, grp], own_sem.at[i])

    for i in range(CHUNKS):
        own_copy(i).start()

        def send(j, carry):
            first_copy(i, lax.rem(chan + j, n_chan)).start()
            return carry

        lax.fori_loop(1, n_chan, send, 0)

    def grp_copy(i, part, owner, to, send_sem, recv_sem):
        if part is None:
            piece = out_ref.at[span(i), :, :, owner]
        else:
            piece = out_ref.at[span(i), pl.ds(part * pols, pols), :, owner]
        return pltpu.make_async_remote_copy(
            src_ref=piece, dst_ref=piece, send_sem=send_sem, recv_sem=recv_sem,
            device_id={"chan": chan, "grp": to}, device_id_type=MESH,
        )

    def side(i, d):
        return grp_copy(i, None, grp, (right, left)[d], side_send.at[i, d], side_recv.at[i, d])

    def side_in(i, d):
        return grp_copy(i, None, (left, right)[d], right, side_send.at[i, d], side_recv.at[i, d])

    def far(i, d):
        return grp_copy(i, d, (left, right)[d], (right, left)[d], far_send.at[i, d], far_recv.at[i, d])

    def far_in(i, d):
        return grp_copy(i, d, across, right, far_send.at[i, d], far_recv.at[i, d])

    def mate_copy(i, e):
        if e == 0:
            return grp_copy(i, None, grp, mate, mate_send.at[i, e], mate_recv.at[i, e])
        if e < 3:
            return grp_copy(i, None, (left, right)[e - 1], mate, mate_send.at[i, e], mate_recv.at[i, e])
        return grp_copy(i, e - 3, across, mate, mate_send.at[i, e], mate_recv.at[i, e])

    def mate_in(i, e):
        shift = 1 - 2 * core
        if e == 0:
            return grp_copy(i, None, mate, mate, mate_send.at[i, e], mate_recv.at[i, e])
        if e < 3:
            return grp_copy(i, None, (left, right)[e - 1] + shift, mate, mate_send.at[i, e], mate_recv.at[i, e])
        return grp_copy(i, e - 3, across + shift, mate, mate_send.at[i, e], mate_recv.at[i, e])

    def gathered(i):
        piece = out_ref.at[span(i), :, pl.ds(0, n_chan - 1), grp]
        return pltpu.make_async_copy(piece, piece, one_recv.at[i])

    def sent(i):
        piece = outgoing.at[pl.ds(0, n_chan - 1), span(i)]
        return pltpu.make_async_copy(piece, piece, one_send.at[i])

    for t in range(CHUNKS + 2):
        if t < CHUNKS:
            own_copy(t).wait()
            gathered(t).wait()
            for d in range(2):
                side(t, d).start()
            mate_copy(t, 0).start()
        i = t - 1
        if 0 <= i < CHUNKS:
            for d in range(2):
                side_in(i, d).wait_recv()
                far(i, d).start()
                mate_copy(i, 1 + d).start()
        i = t - 2
        if 0 <= i < CHUNKS:
            for d in range(2):
                far_in(i, d).wait_recv()
                mate_copy(i, 3 + d).start()
    for i in range(CHUNKS):
        sent(i).wait()
        for d in range(2):
            side(i, d).wait_send()
            far(i, d).wait_send()
        for e in range(5):
            mate_copy(i, e).wait_send()
            mate_in(i, e).wait_recv()


def beams_kernel(dims, weights_ref, spectra_ref, out_ref, wide, ordered, values):
    beams, stations, pols, spectra = dims
    tiles = stations // LANES
    rows_b = 2 * tiles
    group = 64
    for i in range(beams // group):
        wide[pl.ds(i * group * rows_b, group * rows_b), :] = weights_ref[
            pl.ds(i * group * rows_b, group * rows_b), :
        ].astype(jnp.float32)
    for w in range(2):
        for tile in range(tiles):
            ordered[:, pl.ds((w * tiles + tile) * LANES, LANES)] = wide[
                pl.ds(tile * 2 + w, beams, stride=rows_b), :
            ].astype(jnp.bfloat16)
    real = jnp.concatenate([spectra_ref[0, p * 2] for p in range(pols)], axis=1)
    imag = jnp.concatenate([spectra_ref[0, p * 2 + 1] for p in range(pols)], axis=1)
    weights = ordered[...]
    for part in range(2):
        other = jnp.concatenate([imag, real] if part else [real, -imag], axis=0)
        product = jnp.dot(weights, other, preferred_element_type=jnp.float32)
        for p in range(pols):
            values[pl.ds(p * 2 + part, beams, stride=2 * pols), :] = product[:, p * spectra : (p + 1) * spectra]
    out_ref[...] = values[...].astype(jnp.bfloat16)


def shards(sizes, voltages, filter_taps, chan_index, beam_weights):
    n_chan, n_grp = sizes
    stations, pols, blocks, width = voltages.shape
    taps, size = filter_taps.shape
    channels = chan_index.shape[0]
    per, beams = beam_weights.shape[:2]
    everyone = beam_weights.shape[3]
    spectra = blocks - taps + 1
    tiles = size // LANES
    rows_m = 2 * tiles * pols
    quads = 2 * pols

    lines = voltages.transpose(0, 2, 1, 3).reshape(stations, blocks, pols, 2 * tiles, LANES)
    lines = lines.transpose(0, 1, 3, 2, 4).reshape(stations * blocks * rows_m, LANES)
    index = chan_index.reshape(channels, 1)
    dims = (n_chan, n_grp // 2, stations, pols, blocks, taps, size, channels)
    spread_rows = channels * quads * stations
    dma = pltpu.SemaphoreType.DMA
    held = pl.pallas_call(
        functools.partial(spectra_kernel, dims),
        out_shape=jax.ShapeDtypeStruct((per, quads, n_chan, n_grp, stations, LANES), jnp.bfloat16),
        in_specs=[
            pl.BlockSpec(memory_space=pl.ANY),
            pl.BlockSpec(memory_space=pltpu.VMEM),
            pl.BlockSpec(memory_space=pltpu.VMEM),
            pl.BlockSpec(memory_space=pltpu.VMEM),
        ],
        out_specs=pl.BlockSpec(memory_space=pl.ANY),
        scratch_shapes=[
            pltpu.VMEM((stations * blocks * rows_m, LANES), jnp.bfloat16),
            pltpu.VMEM((taps * tiles * pols, LANES), jnp.float32),
            pltpu.VMEM((2 * channels, 2 * size), jnp.bfloat16),
            pltpu.VMEM((spectra * rows_m, LANES), jnp.float32),
            pltpu.VMEM((pols * spectra, 2 * size), jnp.bfloat16),
            pltpu.VMEM((spread_rows, LANES), jnp.float32),
            pltpu.VMEM((spread_rows // stations, stations, LANES), jnp.bfloat16),
            dma((stations,)), dma((CHUNKS,)), dma((CHUNKS,)), dma((CHUNKS,)),
            dma((CHUNKS, 2)), dma((CHUNKS, 2)), dma((CHUNKS, 2)), dma((CHUNKS, 2)),
            dma((CHUNKS, 5)), dma((CHUNKS, 5)),
        ],
        compiler_params=pltpu.CompilerParams(
            collective_id=0, has_side_effects=True, vmem_limit_bytes=48 * 1024 * 1024
        ),
        name="spectra",
    )(lines, filter_taps, index, jnp.asarray(fourier_rows(size)))

    held = held.reshape(per, quads, everyone, LANES)
    tiles_s = everyone // LANES
    rows_w = beam_weights.reshape(per, beams, 2, tiles_s, LANES).transpose(0, 1, 3, 2, 4)
    rows_w = rows_w.reshape(per * beams * tiles_s * 2, LANES)
    beam_rows = beams * tiles_s * 2
    out = pl.pallas_call(
        functools.partial(beams_kernel, (beams, everyone, pols, spectra)),
        out_shape=jax.ShapeDtypeStruct((per * beams * quads, LANES), jnp.bfloat16),
        grid=(per,),
        in_specs=[
            pl.BlockSpec((beam_rows, LANES), lambda k: (k, 0)),
            pl.BlockSpec((1, quads, everyone, LANES), lambda k: (k, 0, 0, 0)),
        ],
        out_specs=pl.BlockSpec((beams * quads, LANES), lambda k: (k, 0)),
        scratch_shapes=[
            pltpu.VMEM((beam_rows, LANES), jnp.float32),
            pltpu.VMEM((beams, 2 * everyone), jnp.bfloat16),
            pltpu.VMEM((beams * quads, LANES), jnp.float32),
        ],
        compiler_params=pltpu.CompilerParams(vmem_limit_bytes=48 * 1024 * 1024),
        name="beams",
    )(rows_w, held)
    return out.reshape(per, beams, pols, 2, spectra)


def solution(mesh):
    sizes = (mesh.shape["chan"], mesh.shape["grp"])
    placed = (P(("chan", "grp"), None, None, None), P(), P(), P("chan", "grp", None, None))
    return jax.shard_map(
        functools.partial(shards, sizes),
        mesh=mesh,
        in_specs=placed,
        out_specs=P("chan", "grp", None, None, None),
        check_vma=False,
    )
```

time: 248 us -> 72.9 us (0.29)
  blocking collectives: 79.1 us -> 0 us
  Pallas kernels: 0 us -> 67.9 us
  local copies, waits for them, and re-layouts: 60 us -> 4.41 us
  waiting for transfers between devices: 48.2 us -> 0 us
  other arithmetic: 26.9 us -> 0 us
  matrix products: 19.4 us -> 0 us
  between operations: 13.4 us -> 0.03 us
    all_to_all x1 -> x0, blocking collectives: 79.1 us -> none  [shards(): lax.all_to_all(gathered, 'chan', split_axis=4, concat_axis=0, tiled=True)]
    pallas_call x0 -> x2, Pallas kernels: none -> 67.9 us  [the longest x1 50.8 us: shards(): pl.pallas_call(functools.partial(spectra_kernel, dims), out_shape=jax.Sha...]
    all_gather x1 -> x0, waiting for transfers between devices: 48.1 us -> none  [shards(): gathered = lax.all_gather(spectra, 'grp', axis=0, tiled=True)]
    slice x2 -> x0, local copies, waits for them, and re-layouts: 26.9 us -> none  [the longest x1 26.8 us: channelize(): voltages[:, :, tap_delay:tap_delay + spectra_count, :].astype(jnp.float32)]
    dot_general x2 -> x0, matrix products: 19.4 us -> none  [the longest x1 16 us: shards(): jnp.einsum('cbws,spmrc->cbwprm', beam_weights, turned, preferred_element_...]
    another operation x1 -> x0, local copies, waits for them, and re-layouts: 16.2 us -> none  [shards(): return jnp.stack([real_part, imag_part], axis=3).astype(jnp.bfloat16)]
    convert_element_type x1 -> x0, other arithmetic: 8.28 us -> none  [channelize(): filtered = filtered.astype(jnp.bfloat16)]
    all_gather x1 -> x0, local copies, waits for them, and re-layouts: 7.05 us -> none  [shards(): gathered = lax.all_gather(spectra, 'grp', axis=0, tiled=True)]
  transfers between devices with their start and end apart: 1 -> 0, of which waited for: 1 -> 0; matrix products, arithmetic and copies ran while one was open for 0% -> 0% of each run, Pallas kernels for 0% -> 0%
where the time goes in v1:
time: 72.9 us; the launch traced here: 72.4 us
  Pallas kernels  67.9 us (93%)
  local copies, waits for them, and re-layouts  4.41 us (6%)
    pallas_call x1, Pallas kernels, shards(): pl.pallas_call(functools.partial(spectra_kernel, dims), out_shape=jax.Sha...  50.8 us
    pallas_call x1, Pallas kernels, shards(): pl.pallas_call(functools.partial(beams_kernel, (beams, everyone, pols, sp...  17.1 us
    unnamed x6, local copies, waits for them, and re-layouts  3.62 us

profile of v1, /device:TPU:1, one launch (start us, length us, event | category | flops | bytes accessed | tf_op | source)
XLA Modules:
  0.0 72.4 jit_solution(8975690025768452379)
XLA Ops:
  0.0 0.8 %copy.10.index_ref = s32[192,1]{1,0:T(8,128)S(1)} copy(s32[192,1]{0,1:T(1,128)} %bitcast.18) | data formatting | bytes 1536 | tf_op jit(solution)/shard_map/reshape | solution.py:267
  0.8 0.0 copy-start
  0.8 1.6 %copy-done = bf16[4,2,139,1024]{3,1,2,0:T(2,128)(2,1)S(1)} copy-done((bf16[4,2,139,1024]{3,1,2,0:T(2,128)(2,1)S(1)}, bf16[4,2,139,1024]{3,1,2,0:T(2,128)(2,1)}, u32[]{:S(2)}) %copy-start) | copy-done | bytes 2277400
  2.4 0.0 copy-start.1
  2.4 1.2 %copy-done.1 = bf16[512,1024]{1,0:T(8,128)(2,1)S(1)} copy-done((bf16[512,1024]{1,0:T(8,128)(2,1)S(1)}, bf16[512,1024]{1,0:T(8,128)(2,1)}, u32[]{:S(2)}) %copy-start.1) | copy-done | bytes 1048600
  3.7 0.0 copy-start.2
  3.7 0.8 %copy-done.2 = f32[12,512]{1,0:T(8,128)S(1)} copy-done((f32[12,512]{1,0:T(8,128)S(1)}, f32[12,512]{1,0:T(8,128)}, u32[]{:S(2)}) %copy-start.2) | copy-done | bytes 24600
  4.4 50.8 %spectra.1 = bf16[12,4,16,8,4,128]{5,4,3,2,1,0:T(4,128)(2,1)} custom-call(bf16[8896,128]{1,0:T(8,128)(2,1)S(1)} %bitcast.15, f32[12,512]{1,0:T(8,128)S(1)} %copy-done.2, s32[192,1]{1,0:T(8,128)S(1)} %copy.10.index_ref, bf16[512,1024]{1,0:T(8,128)(2,1)S(1)} %copy-done.1), custom_call_target="tpu_custom_call" | custom-call | tf_op jit(solution)/shard_map/spectra/pallas_call | solution.py:271
  55.2 17.1 %beams.1 = bf16[24576,128]{1,0:T(8,128)(2,1)} custom-call(bf16[49152,128]{1,0:T(8,128)(2,1)} %bitcast.17, bf16[12,4,512,128]{3,2,1,0:T(8,128)(2,1)} %bitcast.16), custom_call_target="tpu_custom_call" | custom-call | tf_op jit(solution)/shard_map/beams/pallas_call | solution.py:304
Async XLA Ops:
  0.8 1.6 %copy-start = (bf16[4,2,139,1024]{3,1,2,0:T(2,128)(2,1)S(1)}, bf16[4,2,139,1024]{3,1,2,0:T(2,128)(2,1)}, u32[]{:S(2)}) copy-start(bf16[4,2,139,1024]{3,1,2,0:T(2,128)(2,1)} %param.5) | copy-start | bytes 6832132
  2.4 1.2 %copy-start.1 = (bf16[512,1024]{1,0:T(8,128)(2,1)S(1)}, bf16[512,1024]{1,0:T(8,128)(2,1)}, u32[]{:S(2)}) copy-start(bf16[512,1024]{1,0:T(8,128)(2,1)} %constant.2.clone.rows_ref) | copy-start | bytes 3145732
  3.7 0.8 %copy-start.2 = (f32[12,512]{1,0:T(8,128)S(1)}, f32[12,512]{1,0:T(8,128)}, u32[]{:S(2)}) copy-start(f32[12,512]{1,0:T(8,128)} %taps_ref.1) | copy-start | bytes 73732

commit v2 on v1

v2 whole, which is shorter than its diff:
```python
import functools
import math

import jax
import jax.numpy as jnp
import numpy as np
from jax import lax
from jax.experimental import pallas as pl
from jax.experimental.pallas import tpu as pltpu
from jax.sharding import PartitionSpec as P

MESH = pl.DeviceIdType.MESH
LANES = 128
CHUNKS = 6
LATE = 4


def fourier_rows(size):
    steps = np.arange(size, dtype=np.int64)
    phase = (steps[:, None] * steps[None, :]) % size
    angle = np.float32(2.0 * math.pi / size) * phase.astype(np.float32)
    factor = np.float32(1.0 / math.sqrt(size))
    rows = np.concatenate([np.cos(angle) * factor, np.sin(angle) * factor], axis=1)
    return rows.astype(jnp.bfloat16)


def spectra_kernel(
    dims, volts_hbm, taps_hbm, index_ref, rows_hbm, weights_hbm, part_ref, late_ref, late_weights_ref,
    volts, taps_ref, rows_ref, tapb, table, sums, flat, spread, ready, held, raw, wide, ordered, values, done,
    load_sem, own_sem, one_send, one_recv, side_send, side_recv, far_send, far_recv, mate_send, mate_recv,
    raw_sem, part_sem, late_sem, late_weights_sem,
):
    n_chan, n_x, stations, pols, blocks, taps, size, channels, beams, late = dims
    n_grp = 2 * n_x
    spectra = blocks - taps + 1
    tiles = size // LANES
    per = channels // n_chan
    step = per // CHUNKS
    early = per - late
    quads = 2 * pols
    rows_m = 2 * tiles * pols
    everyone = n_chan * n_grp * stations
    tiles_s = everyone // LANES
    rows_b = 2 * tiles_s
    rows_w = beams * rows_b
    rows_o = beams * quads

    chan = lax.axis_index("chan")
    grp = lax.axis_index("grp")
    place = grp // 2
    core = grp % 2
    right = lax.rem(place + 1, n_x) * 2 + core
    left = lax.rem(place + n_x - 1, n_x) * 2 + core
    across = lax.rem(place + 2, n_x) * 2 + core
    mate = place * 2 + 1 - core

    def load(s):
        span = pl.ds(s * blocks * rows_m, blocks * rows_m)
        return pltpu.make_async_copy(volts_hbm.at[span], volts.at[span], load_sem.at[s])

    def load_taps():
        return pltpu.make_async_copy(taps_hbm, taps_ref, load_sem.at[stations])

    def load_rows():
        return pltpu.make_async_copy(rows_hbm, rows_ref, load_sem.at[stations + 1])

    load_taps().start()
    load(0).start()
    load_rows().start()
    for s in range(1, stations):
        load(s).start()

    barrier = pltpu.get_barrier_semaphore()

    def greet(j, carry):
        other = lax.rem(chan + j, n_chan)
        pl.semaphore_signal(barrier, inc=1, device_id={"chan": other, "grp": grp}, device_id_type=MESH)
        return carry

    lax.fori_loop(1, n_chan, greet, 0)
    for other in (right, left, mate):
        pl.semaphore_signal(barrier, inc=1, device_id={"chan": chan, "grp": other}, device_id_type=MESH)

    load_taps().wait()
    for t in range(taps):
        for tile in range(tiles):
            line = taps_ref[pl.ds(t, 1), pl.ds(tile * LANES, LANES)]
            tapb[pl.ds((t * tiles + tile) * pols, pols), :] = jnp.broadcast_to(line, (pols, LANES))

    load_rows().wait()
    place_of = lax.broadcasted_iota(jnp.int32, (size, channels), 0)
    chosen = (place_of == index_ref[...]).astype(jnp.float32).astype(jnp.bfloat16)
    picked = lax.dot_general(
        chosen, rows_ref[...], (((0,), (0,)), ((), ())), preferred_element_type=jnp.float32
    )
    table[pl.ds(0, channels), :] = picked.astype(jnp.bfloat16)
    table[pl.ds(channels, channels), pl.ds(0, size)] = (-picked[:, size:]).astype(jnp.bfloat16)
    table[pl.ds(channels, channels), pl.ds(size, size)] = picked[:, :size].astype(jnp.bfloat16)

    group = 8
    half = tiles * pols
    for s in range(stations):
        load(s).wait()

        def filter_group(i, carry):
            first = i * group
            coefs = [tapb[pl.ds(t * half, half), :] for t in range(taps)]
            views = []
            for m in range(group + taps - 1):
                start = pl.multiple_of((s * blocks + first + m) * rows_m, rows_m)
                views.append(volts[pl.ds(start, rows_m), :].astype(jnp.float32))
            for m in range(group):
                for part in range(2):
                    total = None
                    for t in range(taps):
                        term = views[m + t][part * half : (part + 1) * half] * coefs[t]
                        total = term if total is None else total + term
                    at = pl.multiple_of((first + m) * rows_m, rows_m) + part * half
                    sums[pl.ds(at, half), :] = total
            return carry

        lax.fori_loop(0, spectra // group, filter_group, 0)
        for p in range(pols):
            for part in range(2):
                for tile in range(tiles):
                    line = part * half + tile * pols + p
                    flat[pl.ds(p * spectra, spectra), pl.ds((part * tiles + tile) * LANES, LANES)] = sums[
                        pl.ds(line, spectra, stride=rows_m), :
                    ].astype(jnp.bfloat16)
        product = sum(
            lax.dot_general(
                table[:, part * size : (part + 1) * size],
                flat[:, part * size : (part + 1) * size],
                (((1,), (1,)), ((), ())),
                preferred_element_type=jnp.float32,
            )
            for part in range(2)
        )
        for p in range(pols):
            for part in range(2):
                spread[pl.ds((p * 2 + part) * stations + s, channels, stride=quads * stations), :] = product[
                    part * channels : (part + 1) * channels, p * spectra : (p + 1) * spectra
                ]

    packed = ready.reshape(channels * quads * stations, LANES)

    def pack(k, carry):
        wider = spread[pl.ds(pl.multiple_of(k * 64, 64), 64), :].astype(jnp.bfloat16)
        packed[pl.ds(pl.multiple_of(k * 64, 64), 64), :] = wider
        return carry

    lax.fori_loop(0, channels * quads * stations // 64, pack, 0)

    outgoing = ready.reshape(n_chan, per, quads, stations, LANES)
    pl.semaphore_wait(barrier, n_chan + 2)

    def span(i):
        return pl.ds(i * step, step)

    def first_copy(i, other):
        return pltpu.make_async_remote_copy(
            src_ref=outgoing.at[other, span(i)],
            dst_ref=held.at[span(i), :, chan, grp],
            send_sem=one_send.at[i],
            recv_sem=one_recv.at[i],
            device_id={"chan": other, "grp": grp},
            device_id_type=MESH,
        )

    def own_copy(i):
        return pltpu.make_async_copy(outgoing.at[chan, span(i)], held.at[span(i), :, chan, grp], own_sem.at[i])

    def first_sends(i, carry):
        own_copy(i).start()

        def send(j, carry):
            first_copy(i, lax.rem(chan + j, n_chan)).start()
            return carry

        return lax.fori_loop(1, n_chan, send, carry)

    lax.fori_loop(0, CHUNKS, first_sends, 0)

    def grp_copy(i, part, owner, to, send_sem, recv_sem):
        if part is None:
            piece = held.at[span(i), :, :, owner]
        else:
            piece = held.at[span(i), pl.ds(part * pols, pols), :, owner]
        return pltpu.make_async_remote_copy(
            src_ref=piece, dst_ref=piece, send_sem=send_sem, recv_sem=recv_sem,
            device_id={"chan": chan, "grp": to}, device_id_type=MESH,
        )

    def side(i, d):
        return grp_copy(i, None, grp, (right, left)[d], side_send.at[i, d], side_recv.at[i, d])

    def side_in(i, d):
        return grp_copy(i, None, (left, right)[d], right, side_send.at[i, d], side_recv.at[i, d])

    def far(i, d):
        return grp_copy(i, d, (left, right)[d], (right, left)[d], far_send.at[i, d], far_recv.at[i, d])

    def far_in(i, d):
        return grp_copy(i, d, across, right, far_send.at[i, d], far_recv.at[i, d])

    def mate_copy(i, e):
        sems = (mate_send.at[i, e], mate_recv.at[i, e])
        if e == 0:
            return grp_copy(i, None, grp, mate, *sems)
        if e < 3:
            return grp_copy(i, None, (left, right)[e - 1], mate, *sems)
        return grp_copy(i, e - 3, across, mate, *sems)

    def mate_in(i, e):
        shift = 1 - 2 * core
        sems = (mate_send.at[i, e], mate_recv.at[i, e])
        if e == 0:
            return grp_copy(i, None, mate, mate, *sems)
        if e < 3:
            return grp_copy(i, None, (left, right)[e - 1] + shift, mate, *sems)
        return grp_copy(i, e - 3, across + shift, mate, *sems)

    def gathered(i):
        piece = held.at[span(i), :, pl.ds(0, n_chan - 1), grp]
        return pltpu.make_async_copy(piece, piece, one_recv.at[i])

    def sent(i):
        piece = outgoing.at[pl.ds(0, n_chan - 1), span(i)]
        return pltpu.make_async_copy(piece, piece, one_send.at[i])

    def load_raw(k):
        return pltpu.make_async_copy(
            weights_hbm.at[pl.ds(pl.multiple_of(k * rows_w, rows_w), rows_w)], raw.at[k % 2], raw_sem.at[k % 2]
        )

    def late_weights(k):
        return pltpu.make_async_copy(ordered.at[k], late_weights_ref.at[k - early], late_weights_sem.at[k - early])

    def late_spectra(i):
        where = pl.ds(i * step - early, step)
        return pltpu.make_async_copy(held.at[span(i)], late_ref.at[where], late_sem.at[i])

    def order(k, carry):
        load_raw(k).wait()

        @pl.when(k + 1 < per)
        def _():
            load_raw(k + 1).start()

        wide[...] = raw[k % 2].astype(jnp.float32)
        for w in range(2):
            for tile in range(tiles_s):
                ordered[k, :, pl.ds((w * tiles_s + tile) * LANES, LANES)] = wide[
                    pl.ds(tile * 2 + w, beams, stride=rows_b), :
                ].astype(jnp.bfloat16)

        @pl.when(k >= early)
        def _():
            late_weights(k).start()

        return carry

    lines = held.reshape(per * quads * everyone, LANES)

    def put(k):
        return pltpu.make_async_copy(
            done.at[k % 2], part_ref.at[pl.ds(pl.multiple_of(k * rows_o, rows_o), rows_o)], part_sem.at[k % 2]
        )

    def form(k, carry):
        quad = [
            lines[pl.ds(pl.multiple_of((k * quads + q) * everyone, everyone), everyone), :] for q in range(quads)
        ]
        form_beams(quad, ordered[k], values, beams, pols, spectra)

        @pl.when(k >= 2)
        def _():
            put(k).wait()

        done[k % 2] = values[...].astype(jnp.bfloat16)
        put(k).start()
        return carry

    load_raw(0).start()

    def turn(t, carry):
        @pl.when(t < CHUNKS)
        def _():
            lax.fori_loop(t * step, (t + 1) * step, order, 0)
            own_copy(t).wait()
            gathered(t).wait()
            for d in range(2):
                side(t, d).start()
            mate_copy(t, 0).start()

        @pl.when((t >= 1) & (t < CHUNKS + 1))
        def _():
            for d in range(2):
                side_in(t - 1, d).wait_recv()
                far(t - 1, d).start()
                mate_copy(t - 1, 1 + d).start()

        @pl.when((t >= 2) & (t < CHUNKS + 2))
        def _():
            for d in range(2):
                far_in(t - 2, d).wait_recv()
                mate_copy(t - 2, 3 + d).start()

        @pl.when((t >= 3) & (t < CHUNKS + 3))
        def _():
            for e in range(5):
                mate_in(t - 3, e).wait_recv()

            @pl.when(t - 3 >= early // step)
            def _():
                late_spectra(t - 3).start()

            @pl.when(t - 3 < early // step)
            def _():
                lax.fori_loop((t - 3) * step, (t - 2) * step, form, 0)

        return carry

    lax.fori_loop(0, CHUNKS + 3, turn, 0)

    def finish(i, carry):
        sent(i).wait()
        for d in range(2):
            side(i, d).wait_send()
            far(i, d).wait_send()
        for e in range(5):
            mate_copy(i, e).wait_send()
        return carry

    lax.fori_loop(0, CHUNKS, finish, 0)
    for k in range(early - 2, early):
        put(k).wait()
    for k in range(early, per):
        late_weights(k).wait()
    for i in range(early // step, CHUNKS):
        late_spectra(i).wait()


def form_beams(quad, weights, values, beams, pols, spectra):
    real = jnp.concatenate([quad[p * 2] for p in range(pols)], axis=1)
    imag = jnp.concatenate([quad[p * 2 + 1] for p in range(pols)], axis=1)
    for part in range(2):
        other = jnp.concatenate([imag, real] if part else [real, -imag], axis=0)
        product = jnp.dot(weights, other, preferred_element_type=jnp.float32)
        for p in range(pols):
            values[pl.ds(p * 2 + part, beams, stride=2 * pols), :] = product[:, p * spectra : (p + 1) * spectra]


def beams_kernel(
    dims, part_hbm, spectra_hbm, weights_hbm, out_ref, part, held, ordered, values, done,
    part_in, part_out, held_sem, ordered_sem, done_sem,
):
    beams, pols, spectra, early, late = dims
    quads = 2 * pols
    rows_o = beams * quads

    def take(k):
        where = pl.ds(k * rows_o, rows_o)
        return pltpu.make_async_copy(part_hbm.at[where], part.at[where], part_in.at[k])

    def give(k):
        where = pl.ds(k * rows_o, rows_o)
        return pltpu.make_async_copy(part.at[where], out_ref.at[where], part_out.at[k])

    def spectra_of(k):
        return pltpu.make_async_copy(spectra_hbm.at[k], held.at[k], held_sem.at[k])

    def weights_of(k):
        return pltpu.make_async_copy(weights_hbm.at[k], ordered.at[k], ordered_sem.at[k])

    def put(k):
        return pltpu.make_async_copy(
            done.at[k], out_ref.at[pl.ds((early + k) * rows_o, rows_o)], done_sem.at[k]
        )

    each = -(-early // late)
    for k in range(late):
        spectra_of(k).start()
        weights_of(k).start()
    for k in range(early):
        take(k).start()
    for k in range(late):
        spectra_of(k).wait()
        weights_of(k).wait()
        form_beams([held[k, q] for q in range(quads)], ordered[k], values, beams, pols, spectra)
        done[k] = values[...].astype(jnp.bfloat16)
        put(k).start()
        for j in range(k * each, min(early, (k + 1) * each)):
            take(j).wait()
            give(j).start()
    for k in range(early):
        give(k).wait()
    for k in range(late):
        put(k).wait()


def shards(sizes, voltages, filter_taps, chan_index, beam_weights):
    n_chan, n_grp = sizes
    stations, pols, blocks, width = voltages.shape
    taps, size = filter_taps.shape
    channels = chan_index.shape[0]
    per, beams = beam_weights.shape[:2]
    everyone = beam_weights.shape[3]
    spectra = blocks - taps + 1
    tiles = size // LANES
    tiles_s = everyone // LANES
    rows_m = 2 * tiles * pols
    quads = 2 * pols
    late = LATE
    early = per - late
    beam_rows = beams * tiles_s * 2
    rows_o = beams * quads

    lines = voltages.transpose(0, 2, 1, 3).reshape(stations, blocks, pols, 2 * tiles, LANES)
    lines = lines.transpose(0, 1, 3, 2, 4).reshape(stations * blocks * rows_m, LANES)
    rows_w = beam_weights.reshape(per, beams, 2, tiles_s, LANES).transpose(0, 1, 3, 2, 4)
    rows_w = rows_w.reshape(per * beam_rows, LANES)
    index = chan_index.reshape(1, channels)
    dims = (n_chan, n_grp // 2, stations, pols, blocks, taps, size, channels, beams, late)
    spread_rows = channels * quads * stations
    dma = pltpu.SemaphoreType.DMA
    anywhere = pl.BlockSpec(memory_space=pl.ANY)
    part, held, ordered = pl.pallas_call(
        functools.partial(spectra_kernel, dims),
        out_shape=[
            jax.ShapeDtypeStruct((early * rows_o, LANES), jnp.bfloat16),
            jax.ShapeDtypeStruct((late, quads, n_chan, n_grp, stations, LANES), jnp.bfloat16),
            jax.ShapeDtypeStruct((late, beams, 2 * everyone), jnp.bfloat16),
        ],
        in_specs=[anywhere, anywhere, pl.BlockSpec(memory_space=pltpu.VMEM), anywhere, anywhere],
        out_specs=[anywhere] * 3,
        scratch_shapes=[
            pltpu.VMEM((stations * blocks * rows_m, LANES), jnp.bfloat16),
            pltpu.VMEM((taps, size), jnp.float32),
            pltpu.VMEM((size, 2 * size), jnp.bfloat16),
            pltpu.VMEM((taps * tiles * pols, LANES), jnp.float32),
            pltpu.VMEM((2 * channels, 2 * size), jnp.bfloat16),
            pltpu.VMEM((spectra * rows_m, LANES), jnp.float32),
            pltpu.VMEM((pols * spectra, 2 * size), jnp.bfloat16),
            pltpu.VMEM((spread_rows, LANES), jnp.float32),
            pltpu.VMEM((spread_rows // stations, stations, LANES), jnp.bfloat16),
            pltpu.VMEM((per, quads, n_chan, n_grp, stations, LANES), jnp.bfloat16),
            pltpu.VMEM((2, beam_rows, LANES), jnp.bfloat16),
            pltpu.VMEM((beam_rows, LANES), jnp.float32),
            pltpu.VMEM((per, beams, 2 * everyone), jnp.bfloat16),
            pltpu.VMEM((rows_o, LANES), jnp.float32),
            pltpu.VMEM((2, rows_o, LANES), jnp.bfloat16),
            dma((stations + 2,)), dma((CHUNKS,)), dma((CHUNKS,)), dma((CHUNKS,)),
            dma((CHUNKS, 2)), dma((CHUNKS, 2)), dma((CHUNKS, 2)), dma((CHUNKS, 2)),
            dma((CHUNKS, 5)), dma((CHUNKS, 5)),
            dma((2,)), dma((2,)), dma((CHUNKS,)), dma((late,)),
        ],
        compiler_params=pltpu.CompilerParams(
            collective_id=0, has_side_effects=True, vmem_limit_bytes=63 * 1024 * 1024
        ),
        name="spectra",
    )(lines, filter_taps, index, jnp.asarray(fourier_rows(size)), rows_w)

    out = pl.pallas_call(
        functools.partial(beams_kernel, (beams, pols, spectra, early, late)),
        out_shape=jax.ShapeDtypeStruct((per * rows_o, LANES), jnp.bfloat16),
        in_specs=[anywhere] * 3,
        out_specs=anywhere,
        scratch_shapes=[
            pltpu.VMEM((early * rows_o, LANES), jnp.bfloat16),
            pltpu.VMEM((late, quads, everyone, LANES), jnp.bfloat16),
            pltpu.VMEM((late, beams, 2 * everyone), jnp.bfloat16),
            pltpu.VMEM((rows_o, LANES), jnp.float32),
            pltpu.VMEM((late, rows_o, LANES), jnp.bfloat16),
            dma((early,)), dma((early,)), dma((late,)), dma((late,)), dma((late,)),
        ],
        compiler_params=pltpu.CompilerParams(vmem_limit_bytes=63 * 1024 * 1024),
        name="beams",
    )(part, held.reshape(late, quads, everyone, LANES), ordered)
    return out.reshape(per, beams, pols, 2, spectra)


def solution(mesh):
    sizes = (mesh.shape["chan"], mesh.shape["grp"])
    placed = (P(("chan", "grp"), None, None, None), P(), P(), P("chan", "grp", None, None))
    return jax.shard_map(
        functools.partial(shards, sizes),
        mesh=mesh,
        in_specs=placed,
        out_specs=P("chan", "grp", None, None, None),
        check_vma=False,
    )
```

time: 72.9 us -> 62 us (0.85)
  Pallas kernels: 67.9 us -> 61.6 us
  local copies, waits for them, and re-layouts: 4.41 us -> 0 us
    pallas_call x2, Pallas kernels: 67.9 us -> 61.6 us  [the longest x1 55.1 us: shards(): pl.pallas_call(functools.partial(spectra_kernel, dims), out_shape=[jax.Sh...]
    unnamed x6 -> x0, local copies, waits for them, and re-layouts: 3.62 us -> none
    reshape x1 -> x0, local copies, waits for them, and re-layouts: 0.79 us -> none  [shards(): index = chan_index.reshape(channels, 1)]
where the time goes in v2:
time: 62 us; the launch traced here: 61.6 us
  Pallas kernels  61.6 us (99%)
    pallas_call x1, Pallas kernels, shards(): pl.pallas_call(functools.partial(spectra_kernel, dims), out_shape=[jax.Sh...  55.1 us
    pallas_call x1, Pallas kernels, shards(): pl.pallas_call(functools.partial(beams_kernel, (beams, pols, spectra, ear...  6.47 us

profile of v2, /device:TPU:1, one launch (start us, length us, event | category | flops | bytes accessed | tf_op | source)
XLA Modules:
  0.0 61.6 jit_solution(16856298520823288919)
XLA Ops:
  0.0 55.1 %spectra.1 = (bf16[16384,128]{1,0:T(8,128)(2,1)}, bf16[4,4,16,8,4,128]{5,4,3,2,1,0:T(4,128)(2,1)}, bf16[4,512,1024]{2,1,0:T(8,128)(2,1)}) custom-call(bf16[8896,128]{1,0:T(8,128)(2,1)} %bitcast.16, f32[12,512]{1,0:T(8,128)} %taps_hbm.1, s32[1,192]{1,0:T(1,128)} %bitcast.18, bf16[512,1024]{1,0:T(8,128)(2,1)} %constant.2.clone.rows_hbm, ...), custom_call_target="tpu_custom_call" | custom-call | tf_op jit(solution)/shard_map/spectra/pallas_call | solution.py:428
  55.2 6.5 %beams.1 = bf16[24576,128]{1,0:T(8,128)(2,1)} custom-call(bf16[16384,128]{1,0:T(8,128)(2,1)} %get-tuple-element.8.part_hbm, bf16[4,4,512,128]{3,2,1,0:T(8,128)(2,1)} %bitcast.17, bf16[4,512,1024]{2,1,0:T(8,128)(2,1)} %get-tuple-element.10.weights_hbm), custom_call_target="tpu_custom_call" | custom-call | tf_op jit(solution)/shard_map/beams/pallas_call | solution.py:464

commit v3 on v2

--- a/solution.py
+++ b/solution.py
@@ -11,7 +11,20 @@
 
 MESH = pl.DeviceIdType.MESH
 LANES = 128
-CHUNKS = 6
+ITEMS = ((0, 2), (2, 4), (4, 6), (6, 8), (8, 10), (10, 12))
+AHEAD = (0, 1)
+TURNS = (
+    (("out", 0), ("first", 2), ("out", 1), ("first", 3)),
+    (("far", 0), ("out", 2), ("first", 4)),
+    (("far", 1), ("out", 3), ("first", 5), ("mate", 0)),
+    (("far", 2), ("out", 4), ("mate", 1), ("all", 0)),
+    (("far", 3), ("out", 5), ("mate", 2), ("all", 1)),
+    (("far", 4), ("mate", 3), ("all", 2)),
+    (("far", 5), ("mate", 4), ("all", 3)),
+    (("mate", 5), ("late", 4), ("late", 5)),
+)
+FORMED = (0, 0, 0, 2, 2, 2, 2, 0)
+ORDERED = (2, 4, 4, 2, 0, 0, 0, 0)
 LATE = 4
 
 
@@ -35,7 +48,6 @@
     spectra = blocks - taps + 1
     tiles = size // LANES
     per = channels // n_chan
-    step = per // CHUNKS
     early = per - late
     quads = 2 * pols
     rows_m = 2 * tiles * pols
@@ -69,6 +81,13 @@
     load_rows().start()
     for s in range(1, stations):
         load(s).start()
+
+    def load_raw(k):
+        return pltpu.make_async_copy(
+            weights_hbm.at[pl.ds(pl.multiple_of(k * rows_w, rows_w), rows_w)], raw.at[k % 2], raw_sem.at[k % 2]
+        )
+
+    load_raw(0).start(priority=1)
 
     barrier = pltpu.get_barrier_semaphore()
 
@@ -97,6 +116,110 @@
     table[pl.ds(channels, channels), pl.ds(0, size)] = (-picked[:, size:]).astype(jnp.bfloat16)
     table[pl.ds(channels, channels), pl.ds(size, size)] = picked[:, :size].astype(jnp.bfloat16)
 
+    outgoing = ready.reshape(n_chan, per, quads, stations, LANES)
+    packed = ready.reshape(channels * quads * stations, LANES)
+
+    def span(i):
+        return pl.ds(ITEMS[i][0], ITEMS[i][1] - ITEMS[i][0])
+
+    def first_copy(i, other):
+        return pltpu.make_async_remote_copy(
+            src_ref=outgoing.at[other, span(i)],
+            dst_ref=held.at[span(i), :, chan, grp],
+            send_sem=one_send.at[i],
+            recv_sem=one_recv.at[i],
+            device_id={"chan": other, "grp": grp},
+            device_id_type=MESH,
+        )
+
+    def own_copy(i):
+        return pltpu.make_async_copy(outgoing.at[chan, span(i)], held.at[span(i), :, chan, grp], own_sem.at[i])
+
+    def first_sends(i):
+        def send(j, carry):
+            first_copy(i, lax.rem(chan + j, n_chan)).start()
+            return carry
+
+        lax.fori_loop(1, n_chan, send, 0)
+        own_copy(i).start()
+
+    def gathered(i):
+        piece = held.at[span(i), :, pl.ds(0, n_chan - 1), grp]
+        return pltpu.make_async_copy(piece, piece, one_recv.at[i])
+
+    def sent(i):
+        piece = held.at[span(i), :, pl.ds(0, n_chan - 1), grp]
+        return pltpu.make_async_copy(piece, piece, one_send.at[i])
+
+    def grp_copy(i, part, owner, to, send_sem, recv_sem):
+        quad = slice(None) if part is None else pl.ds(part * pols, pols)
+        piece = held.at[span(i), quad, :, owner]
+        return pltpu.make_async_remote_copy(
+            src_ref=piece, dst_ref=piece, send_sem=send_sem, recv_sem=recv_sem,
+            device_id={"chan": chan, "grp": to}, device_id_type=MESH,
+        )
+
+    def side(i, d):
+        return grp_copy(i, None, grp, (right, left)[d], side_send.at[i, d], side_recv.at[i, d])
+
+    def side_in(i, d):
+        return grp_copy(i, None, (left, right)[d], right, side_send.at[i, d], side_recv.at[i, d])
+
+    def far(i, d):
+        return grp_copy(i, d, (left, right)[d], (right, left)[d], far_send.at[i, d], far_recv.at[i, d])
+
+    def far_in(i, d):
+        return grp_copy(i, d, across, right, far_send.at[i, d], far_recv.at[i, d])
+
+    def mate_copy(i, e):
+        sems = (mate_send.at[i, e], mate_recv.at[i, e])
+        if e == 0:
+            return grp_copy(i, None, grp, mate, *sems)
+        if e < 3:
+            return grp_copy(i, None, (left, right)[e - 1], mate, *sems)
+        return grp_copy(i, e - 3, across, mate, *sems)
+
+    def mate_in(i, e):
+        shift = 1 - 2 * core
+        sems = (mate_send.at[i, e], mate_recv.at[i, e])
+        if e == 0:
+            return grp_copy(i, None, mate, mate, *sems)
+        if e < 3:
+            return grp_copy(i, None, (left, right)[e - 1] + shift, mate, *sems)
+        return grp_copy(i, e - 3, across + shift, mate, *sems)
+
+    def late_spectra(i):
+        low, high = ITEMS[i]
+        return pltpu.make_async_copy(
+            held.at[pl.ds(low, high - low)], late_ref.at[pl.ds(low - early, high - low)], late_sem.at[i]
+        )
+
+    def out(i):
+        own_copy(i).wait()
+        gathered(i).wait()
+        for d in range(2):
+            side(i, d).start()
+        mate_copy(i, 0).start()
+
+    def act(what, i):
+        if what == "out":
+            out(i)
+        if what == "first":
+            first_sends(i)
+        for d in range(2):
+            if what == "far":
+                side_in(i, d).wait_recv()
+                far(i, d).start()
+                mate_copy(i, 1 + d).start()
+            if what == "mate":
+                far_in(i, d).wait_recv()
+                mate_copy(i, 3 + d).start()
+        if what in ("all", "late"):
+            for e in range(5):
+                mate_in(i, e).wait_recv()
+        if what == "late":
+            late_spectra(i).start(priority=1)
+
     group = 8
     half = tiles * pols
     for s in range(stations):
@@ -109,14 +232,26 @@
             for m in range(group + taps - 1):
                 start = pl.multiple_of((s * blocks + first + m) * rows_m, rows_m)
                 views.append(volts[pl.ds(start, rows_m), :].astype(jnp.float32))
-            for m in range(group):
-                for part in range(2):
-                    total = None
-                    for t in range(taps):
-                        term = views[m + t][part * half : (part + 1) * half] * coefs[t]
-                        total = term if total is None else total + term
-                    at = pl.multiple_of((first + m) * rows_m, rows_m) + part * half
-                    sums[pl.ds(at, half), :] = total
+            both = [coefs[2 * j] + coefs[2 * j + 1] for j in range(taps // 2)]
+            for part in range(2):
+                side_of = [view[part * half : (part + 1) * half] for view in views]
+
+                def chain(values, factors):
+                    total = values[0] * factors[0]
+                    for value, factor in zip(values[1:], factors[1:]):
+                        total = total + value * factor
+                    return total
+
+                joined = [side_of[m] + side_of[m + 1] for m in range(1, group + taps - 2, 2)]
+                before_it = chain(side_of[0 : taps : 2], coefs[0::2])
+                for i in range(group // 2):
+                    odd = chain(side_of[2 * i + 1 : 2 * i + 1 + taps : 2], coefs[1::2])
+                    after_it = chain(side_of[2 * i + 2 : 2 * i + 2 + taps : 2][: taps // 2], coefs[0::2])
+                    cross = chain(joined[i : i + taps // 2], both)
+                    for m, total in ((0, before_it + odd), (1, (cross - odd) - after_it)):
+                        at = pl.multiple_of((first + 2 * i + m) * rows_m, rows_m) + part * half
+                        sums[pl.ds(at, half), :] = total
+                    before_it = after_it
             return carry
 
         lax.fori_loop(0, spectra // group, filter_group, 0)
@@ -142,110 +277,25 @@
                     part * channels : (part + 1) * channels, p * spectra : (p + 1) * spectra
                 ]
 
-    packed = ready.reshape(channels * quads * stations, LANES)
-
     def pack(k, carry):
         wider = spread[pl.ds(pl.multiple_of(k * 64, 64), 64), :].astype(jnp.bfloat16)
         packed[pl.ds(pl.multiple_of(k * 64, 64), 64), :] = wider
         return carry
 
     lax.fori_loop(0, channels * quads * stations // 64, pack, 0)
-
-    outgoing = ready.reshape(n_chan, per, quads, stations, LANES)
     pl.semaphore_wait(barrier, n_chan + 2)
-
-    def span(i):
-        return pl.ds(i * step, step)
-
-    def first_copy(i, other):
-        return pltpu.make_async_remote_copy(
-            src_ref=outgoing.at[other, span(i)],
-            dst_ref=held.at[span(i), :, chan, grp],
-            send_sem=one_send.at[i],
-            recv_sem=one_recv.at[i],
-            device_id={"chan": other, "grp": grp},
-            device_id_type=MESH,
-        )
-
-    def own_copy(i):
-        return pltpu.make_async_copy(outgoing.at[chan, span(i)], held.at[span(i), :, chan, grp], own_sem.at[i])
-
-    def first_sends(i, carry):
-        own_copy(i).start()
-
-        def send(j, carry):
-            first_copy(i, lax.rem(chan + j, n_chan)).start()
-            return carry
-
-        return lax.fori_loop(1, n_chan, send, carry)
-
-    lax.fori_loop(0, CHUNKS, first_sends, 0)
-
-    def grp_copy(i, part, owner, to, send_sem, recv_sem):
-        if part is None:
-            piece = held.at[span(i), :, :, owner]
-        else:
-            piece = held.at[span(i), pl.ds(part * pols, pols), :, owner]
-        return pltpu.make_async_remote_copy(
-            src_ref=piece, dst_ref=piece, send_sem=send_sem, recv_sem=recv_sem,
-            device_id={"chan": chan, "grp": to}, device_id_type=MESH,
-        )
-
-    def side(i, d):
-        return grp_copy(i, None, grp, (right, left)[d], side_send.at[i, d], side_recv.at[i, d])
-
-    def side_in(i, d):
-        return grp_copy(i, None, (left, right)[d], right, side_send.at[i, d], side_recv.at[i, d])
-
-    def far(i, d):
-        return grp_copy(i, d, (left, right)[d], (right, left)[d], far_send.at[i, d], far_recv.at[i, d])
-
-    def far_in(i, d):
-        return grp_copy(i, d, across, right, far_send.at[i, d], far_recv.at[i, d])
-
-    def mate_copy(i, e):
-        sems = (mate_send.at[i, e], mate_recv.at[i, e])
-        if e == 0:
-            return grp_copy(i, None, grp, mate, *sems)
-        if e < 3:
-            return grp_copy(i, None, (left, right)[e - 1], mate, *sems)
-        return grp_copy(i, e - 3, across, mate, *sems)
-
-    def mate_in(i, e):
-        shift = 1 - 2 * core
-        sems = (mate_send.at[i, e], mate_recv.at[i, e])
-        if e == 0:
-            return grp_copy(i, None, mate, mate, *sems)
-        if e < 3:
-            return grp_copy(i, None, (left, right)[e - 1] + shift, mate, *sems)
-        return grp_copy(i, e - 3, across + shift, mate, *sems)
-
-    def gathered(i):
-        piece = held.at[span(i), :, pl.ds(0, n_chan - 1), grp]
-        return pltpu.make_async_copy(piece, piece, one_recv.at[i])
-
-    def sent(i):
-        piece = outgoing.at[pl.ds(0, n_chan - 1), span(i)]
-        return pltpu.make_async_copy(piece, piece, one_send.at[i])
-
-    def load_raw(k):
-        return pltpu.make_async_copy(
-            weights_hbm.at[pl.ds(pl.multiple_of(k * rows_w, rows_w), rows_w)], raw.at[k % 2], raw_sem.at[k % 2]
-        )
+    for i in AHEAD:
+        first_sends(i)
 
     def late_weights(k):
         return pltpu.make_async_copy(ordered.at[k], late_weights_ref.at[k - early], late_weights_sem.at[k - early])
 
-    def late_spectra(i):
-        where = pl.ds(i * step - early, step)
-        return pltpu.make_async_copy(held.at[span(i)], late_ref.at[where], late_sem.at[i])
-
     def order(k, carry):
         load_raw(k).wait()
 
         @pl.when(k + 1 < per)
         def _():
-            load_raw(k + 1).start()
+            load_raw(k + 1).start(priority=1)
 
         wide[...] = raw[k % 2].astype(jnp.float32)
         for w in range(2):
@@ -256,7 +306,7 @@
 
         @pl.when(k >= early)
         def _():
-            late_weights(k).start()
+            late_weights(k).start(priority=1)
 
         return carry
 
@@ -278,67 +328,40 @@
             put(k).wait()
 
         done[k % 2] = values[...].astype(jnp.bfloat16)
-        put(k).start()
+        put(k).start(priority=1)
         return carry
 
-    load_raw(0).start()
-
-    def turn(t, carry):
-        @pl.when(t < CHUNKS)
-        def _():
-            lax.fori_loop(t * step, (t + 1) * step, order, 0)
-            own_copy(t).wait()
-            gathered(t).wait()
-            for d in range(2):
-                side(t, d).start()
-            mate_copy(t, 0).start()
-
-        @pl.when((t >= 1) & (t < CHUNKS + 1))
-        def _():
-            for d in range(2):
-                side_in(t - 1, d).wait_recv()
-                far(t - 1, d).start()
-                mate_copy(t - 1, 1 + d).start()
-
-        @pl.when((t >= 2) & (t < CHUNKS + 2))
-        def _():
-            for d in range(2):
-                far_in(t - 2, d).wait_recv()
-                mate_copy(t - 2, 3 + d).start()
-
-        @pl.when((t >= 3) & (t < CHUNKS + 3))
-        def _():
-            for e in range(5):
-                mate_in(t - 3, e).wait_recv()
-
-            @pl.when(t - 3 >= early // step)
-            def _():
-                late_spectra(t - 3).start()
-
-            @pl.when(t - 3 < early // step)
-            def _():
-                lax.fori_loop((t - 3) * step, (t - 2) * step, form, 0)
-
+    def before(amounts, u):
+        return sum((n * (u > at).astype(jnp.int32) for at, n in enumerate(amounts) if n), jnp.int32(0))
+
+    def turn(u, carry):
+        for at, acts in enumerate(TURNS):
+            if acts:
+
+                @pl.when(u == at)
+                def _():
+                    for what, i in acts:
+                        act(what, i)
+
+        lax.fori_loop(before(ORDERED, u), before(ORDERED, u + 1), order, 0)
+        lax.fori_loop(before(FORMED, u), before(FORMED, u + 1), form, 0)
         return carry
 
-    lax.fori_loop(0, CHUNKS + 3, turn, 0)
-
-    def finish(i, carry):
+    lax.fori_loop(0, len(TURNS), turn, 0)
+    for i in range(len(ITEMS)):
         sent(i).wait()
         for d in range(2):
             side(i, d).wait_send()
             far(i, d).wait_send()
         for e in range(5):
             mate_copy(i, e).wait_send()
-        return carry
-
-    lax.fori_loop(0, CHUNKS, finish, 0)
     for k in range(early - 2, early):
         put(k).wait()
     for k in range(early, per):
         late_weights(k).wait()
-    for i in range(early // step, CHUNKS):
-        late_spectra(i).wait()
+    for i in range(len(ITEMS)):
+        if ITEMS[i][0] >= early:
+            late_spectra(i).wait()
 
 
 def form_beams(quad, weights, values, beams, pols, spectra):
@@ -412,6 +435,7 @@
     rows_m = 2 * tiles * pols
     quads = 2 * pols
     late = LATE
+    items = len(ITEMS)
     early = per - late
     beam_rows = beams * tiles_s * 2
     rows_o = beams * quads
@@ -450,10 +474,10 @@
             pltpu.VMEM((per, beams, 2 * everyone), jnp.bfloat16),
             pltpu.VMEM((rows_o, LANES), jnp.float32),
             pltpu.VMEM((2, rows_o, LANES), jnp.bfloat16),
-            dma((stations + 2,)), dma((CHUNKS,)), dma((CHUNKS,)), dma((CHUNKS,)),
-            dma((CHUNKS, 2)), dma((CHUNKS, 2)), dma((CHUNKS, 2)), dma((CHUNKS, 2)),
-            dma((CHUNKS, 5)), dma((CHUNKS, 5)),
-            dma((2,)), dma((2,)), dma((CHUNKS,)), dma((late,)),
+            dma((stations + 2,)), dma((items,)), dma((items,)), dma((items,)),
+            dma((items, 2)), dma((items, 2)), dma((items, 2)), dma((items, 2)),
+            dma((items, 5)), dma((items, 5)),
+            dma((2,)), dma((2,)), dma((items,)), dma((late,)),
         ],
         compiler_params=pltpu.CompilerParams(
             collective_id=0, has_side_effects=True, vmem_limit_bytes=63 * 1024 * 1024

time: 62 us -> 61 us (0.984)
  Pallas kernels: 61.6 us -> 60.5 us
    pallas_call x1, Pallas kernels: 55.1 us -> 54.1 us  [shards(): pl.pallas_call(functools.partial(spectra_kernel, dims), out_shape=[jax.Sh...]
where the time goes in v3:
time: 61 us; the launch traced here: 60.5 us
  Pallas kernels  60.5 us (99%)
    pallas_call x1, Pallas kernels, shards(): pl.pallas_call(functools.partial(spectra_kernel, dims), out_shape=[jax.Sh...  54.1 us
    pallas_call x1, Pallas kernels, shards(): pl.pallas_call(functools.partial(beams_kernel, (beams, pols, spectra, ear...  6.46 us

profile of v3, /device:TPU:1, one launch (start us, length us, event | category | flops | bytes accessed | tf_op | source)
XLA Modules:
  0.0 60.5 jit_solution(4064865251390230285)
XLA Ops:
  0.0 54.1 %spectra.1 = (bf16[16384,128]{1,0:T(8,128)(2,1)}, bf16[4,4,16,8,4,128]{5,4,3,2,1,0:T(4,128)(2,1)}, bf16[4,512,1024]{2,1,0:T(8,128)(2,1)}) custom-call(bf16[8896,128]{1,0:T(8,128)(2,1)} %bitcast.16, f32[12,512]{1,0:T(8,128)} %taps_hbm.1, s32[1,192]{1,0:T(1,128)} %bitcast.18, bf16[512,1024]{1,0:T(8,128)(2,1)} %constant.2.clone.rows_hbm, ...), custom_call_target="tpu_custom_call" | custom-call | tf_op jit(solution)/shard_map/spectra/pallas_call | solution.py:452
  54.1 6.5 %beams.1 = bf16[24576,128]{1,0:T(8,128)(2,1)} custom-call(bf16[16384,128]{1,0:T(8,128)(2,1)} %get-tuple-element.8.part_hbm, bf16[4,4,512,128]{3,2,1,0:T(8,128)(2,1)} %bitcast.17, bf16[4,512,1024]{2,1,0:T(8,128)(2,1)} %get-tuple-element.10.weights_hbm), custom_call_target="tpu_custom_call" | custom-call | tf_op jit(solution)/shard_map/beams/pallas_call | solution.py:488

commit v4 on v3

--- a/solution.py
+++ b/solution.py
@@ -117,7 +117,7 @@
     table[pl.ds(channels, channels), pl.ds(size, size)] = picked[:, :size].astype(jnp.bfloat16)
 
     outgoing = ready.reshape(n_chan, per, quads, stations, LANES)
-    packed = ready.reshape(channels * quads * stations, LANES)
+    flat_spread = spread.reshape(quads * channels * stations, LANES)
 
     def span(i):
         return pl.ds(ITEMS[i][0], ITEMS[i][1] - ITEMS[i][0])
@@ -249,8 +249,11 @@
                     after_it = chain(side_of[2 * i + 2 : 2 * i + 2 + taps : 2][: taps // 2], coefs[0::2])
                     cross = chain(joined[i : i + taps // 2], both)
                     for m, total in ((0, before_it + odd), (1, (cross - odd) - after_it)):
-                        at = pl.multiple_of((first + 2 * i + m) * rows_m, rows_m) + part * half
-                        sums[pl.ds(at, half), :] = total
+                        for j in range(half // 4):
+                            at = pl.multiple_of(first * 4, group * 4) + (
+                                (part * (half // 4) + j) * spectra + 2 * i + m
+                            ) * 4
+                            sums[pl.ds(at, 4), :] = total[j * 4 : (j + 1) * 4]
                     before_it = after_it
             return carry
 
@@ -259,8 +262,9 @@
             for part in range(2):
                 for tile in range(tiles):
                     line = part * half + tile * pols + p
+                    line = line // 4 * spectra * 4 + line % 4
                     flat[pl.ds(p * spectra, spectra), pl.ds((part * tiles + tile) * LANES, LANES)] = sums[
-                        pl.ds(line, spectra, stride=rows_m), :
+                        pl.ds(line, spectra, stride=4), :
                     ].astype(jnp.bfloat16)
         product = sum(
             lax.dot_general(
@@ -273,16 +277,20 @@
         )
         for p in range(pols):
             for part in range(2):
-                spread[pl.ds((p * 2 + part) * stations + s, channels, stride=quads * stations), :] = product[
+                line = (p * 2 + part) * channels * stations + s
+                flat_spread[pl.ds(line, channels, stride=stations), :] = product[
                     part * channels : (part + 1) * channels, p * spectra : (p + 1) * spectra
                 ]
 
+    by_channel = ready.reshape(channels, quads, stations, LANES)
+
     def pack(k, carry):
-        wider = spread[pl.ds(pl.multiple_of(k * 64, 64), 64), :].astype(jnp.bfloat16)
-        packed[pl.ds(pl.multiple_of(k * 64, 64), 64), :] = wider
+        where = pl.ds(pl.multiple_of(k * 16, 16), 16)
+        for q in range(quads):
+            by_channel[where, q] = spread[q, where].astype(jnp.bfloat16)
         return carry
 
-    lax.fori_loop(0, channels * quads * stations // 64, pack, 0)
+    lax.fori_loop(0, channels // 16, pack, 0)
     pl.semaphore_wait(barrier, n_chan + 2)
     for i in AHEAD:
         first_sends(i)
@@ -466,7 +474,7 @@
             pltpu.VMEM((2 * channels, 2 * size), jnp.bfloat16),
             pltpu.VMEM((spectra * rows_m, LANES), jnp.float32),
             pltpu.VMEM((pols * spectra, 2 * size), jnp.bfloat16),
-            pltpu.VMEM((spread_rows, LANES), jnp.float32),
+            pltpu.VMEM((quads, channels, stations, LANES), jnp.float32),
             pltpu.VMEM((spread_rows // stations, stations, LANES), jnp.bfloat16),
             pltpu.VMEM((per, quads, n_chan, n_grp, stations, LANES), jnp.bfloat16),
             pltpu.VMEM((2, beam_rows, LANES), jnp.bfloat16),

time: 61 us -> 60.4 us (level)
    pallas_call x1, Pallas kernels: 54.1 us -> 53.4 us  [shards(): pl.pallas_call(functools.partial(spectra_kernel, dims), out_shape=[jax.Sh...]
where the time goes in v4:
time: 60.4 us; the launch traced here: 59.9 us
  Pallas kernels  59.9 us (99%)
    pallas_call x1, Pallas kernels, shards(): pl.pallas_call(functools.partial(spectra_kernel, dims), out_shape=[jax.Sh...  53.4 us
    pallas_call x1, Pallas kernels, shards(): pl.pallas_call(functools.partial(beams_kernel, (beams, pols, spectra, ear...  6.47 us

profile of v4, /device:TPU:1, one launch (start us, length us, event | category | flops | bytes accessed | tf_op | source)
XLA Modules:
  0.0 59.9 jit_solution(10961494631177201911)
XLA Ops:
  0.0 53.4 %spectra.1 = (bf16[16384,128]{1,0:T(8,128)(2,1)}, bf16[4,4,16,8,4,128]{5,4,3,2,1,0:T(4,128)(2,1)}, bf16[4,512,1024]{2,1,0:T(8,128)(2,1)}) custom-call(bf16[8896,128]{1,0:T(8,128)(2,1)} %bitcast.16, f32[12,512]{1,0:T(8,128)} %taps_hbm.1, s32[1,192]{1,0:T(1,128)} %bitcast.18, bf16[512,1024]{1,0:T(8,128)(2,1)} %constant.2.clone.rows_hbm, ...), custom_call_target="tpu_custom_call" | custom-call | tf_op jit(solution)/shard_map/spectra/pallas_call | solution.py:460
  53.4 6.5 %beams.1 = bf16[24576,128]{1,0:T(8,128)(2,1)} custom-call(bf16[16384,128]{1,0:T(8,128)(2,1)} %get-tuple-element.8.part_hbm, bf16[4,4,512,128]{3,2,1,0:T(8,128)(2,1)} %bitcast.17, bf16[4,512,1024]{2,1,0:T(8,128)(2,1)} %get-tuple-element.10.weights_hbm), custom_call_target="tpu_custom_call" | custom-call | tf_op jit(solution)/shard_map/beams/pallas_call | solution.py:496
